TPU v7x, 512 devices: a whole 4x4x16 slice. The times are simulated.
512 devices in a mesh: row: 16 (over x, y), col: 32 (over z, core).
Axes of the slice: x: 4, y: 4, z: 16, core: 2. Of those that a mesh axis runs over, the one named last changes fastest.
Arguments:
- rhs: float32 [6144, 12288], P('row', 'col'), may hold values from -6 to 6
- a_pair: float32 [6144, 24576], P('row', 'col'), may hold values from -0.15625 to 0.15625
- b_pair: float32 [12288, 12288], P('row', 'col'), may hold values from -0.15625 to 0.15625
- u_cay: float32 [6144, 384], P('row'), may hold values from -1 to 1, as said below
- v_cay: float32 [384, 12288], P(None, 'col'), may hold values from -1 to 1, as said below
Outputs:
- solved: float32 [6144, 12288], P('row', 'col')
Inputs may be any that keep to these rules, and one draw needn't show every extreme that they name: `u_cay`: each 384 x 384 block of rows has spectral radius below 1. `v_cay`: each 384 x 384 block of columns has spectral radius below 1.
All inputs are finite; a program needn't handle non-finite values.
Results may differ from a plain program's by a relative error of at most 0.0001.
Values sent between devices are 32-bit elements; how exact they have to be, the bound alone decides.
No kernel may reach another device: no remote copies, remote signals or barrier semaphores. Data moves between devices by JAX's collectives and lax.ppermute only.
A program may use at most 64 MiB of HBM per device.

v0:
```python
import jax
import jax.numpy as jnp
from jax import lax
from jax.sharding import PartitionSpec as P

ITERS = 3
precise = lax.Precision.HIGHEST


def from_root(value, axis, source):
    kept = jnp.where(lax.axis_index(axis) == source, value, 0).astype(value.dtype)
    return lax.psum(kept, axis)


def product(left_side, right_side):
    return jnp.dot(left_side, right_side, precision=precise, preferred_element_type=jnp.float32)


def powers(matrix):
    result = [matrix]
    for step_index in range(ITERS - 1):
        result.append(product(result[-1], result[-1]))
    return result


def doubling(u_powers, v_powers, right_side):
    scaled = right_side + product(u_powers[0], right_side)
    iterate = 0.5 * (scaled + product(scaled, v_powers[0]))
    for u_power, v_power in zip(u_powers, v_powers):
        iterate = iterate + product(u_power, product(iterate, v_power))
    return iterate


def body(rhs, a_pair, b_pair, u_cay, v_cay):
    row_index = lax.axis_index("row")
    col_index = lax.axis_index("col")
    row_count = lax.axis_size("row")
    front_sum = lax.axis_size("row") - 1
    block_sum = row_index + col_index
    block_order = rhs.shape[0]
    a_first = a_pair[:, :block_order]
    a_second = a_pair[:, block_order:]
    b_first = b_pair[:block_order]
    b_second = b_pair[block_order:]
    on_first = block_sum == front_sum
    on_second = block_sum == front_sum + 1
    on_trail = block_sum >= front_sum + 2
    empty = jnp.zeros_like(rhs)
    first_x = lax.cond(on_first, lambda: doubling(powers(u_cay), powers(v_cay), rhs), lambda: empty)
    first_down = jax.tree.map(
        lambda part: from_root(part, "row", jnp.clip(front_sum - col_index, 0, row_count - 1)),
        first_x,
    )
    first_across = jax.tree.map(lambda part: from_root(part, "col", front_sum - row_index), first_x)
    from_above = first_down
    from_above = jnp.where(row_index >= 1, from_above, empty)

    def solve_second():
        u_powers, v_powers = (powers(u_cay), powers(v_cay))
        right_side = rhs - (product(a_first, from_above) + product(first_across, b_first))
        return doubling(u_powers, v_powers, right_side)

    second_x = lax.cond(on_second, solve_second, lambda: empty)
    down_root = jnp.clip(front_sum + 1 - col_index, 0, row_count - 1)
    across_root = front_sum + 1 - row_index
    down_pair = (first_down, jax.tree.map(lambda part: from_root(part, "row", down_root), second_x))
    across_pair = (
        first_across,
        jax.tree.map(lambda part: from_root(part, "col", across_root), second_x),
    )
    first_valid = (front_sum - col_index >= 0) & (front_sum - col_index < row_count)
    second_valid = (front_sum + 1 - col_index >= 0) & (front_sum + 1 - col_index < row_count)

    def update_trail():
        upper_first = jnp.where(first_valid, down_pair[0], empty)
        upper_second = jnp.where(second_valid, down_pair[1], empty)
        a_term = product(a_first, upper_first) + product(a_second, upper_second)
        b_term = product(across_pair[0], b_first) + product(across_pair[1], b_second)
        return rhs - (a_term + b_term)

    tail = lax.cond(on_trail, update_trail, lambda: rhs)
    return jnp.where(on_first, first_x, jnp.where(on_second, second_x, tail))


def solution(mesh):
    placed = (P("row", "col"), P("row", "col"), P("row", "col"), P("row", None), P(None, "col"))
    return jax.shard_map(
        body, mesh=mesh, in_specs=placed, out_specs=P("row", "col"), check_vma=False
    )
```

profile of v0, /device:TPU:102, one launch (start us, length us, event | category | flops | bytes accessed | tf_op | source)
XLA Modules:
  0.0 715.6 jit_solution(4404233032780703714)
XLA Ops:
  6.5 0.0 copy-start.1
  6.5 0.0 copy-start
  6.5 0.0 all-reduce.7.cloned.1.call-start
  6.5 1.2 copy.43
  7.7 0.1 copy-done.1
  7.8 0.2 copy-done
  8.0 9.1 %conditional.3 = (f32[384,384]{1,0:T(8,128)S(1)}) conditional(s32[]{:T(128)} %convert_element_type.14, () %tuple.25, (f32[384,384]{1,0:T(8,128)S(1)}, f32[384,384]{1,0:T(8,128)S(1)}, f32[384,384]{1,0:T(8,128)S(1)}) %tuple.59), branch_computations={%region_0.0_spmd, %region_1.0_spmd} | conditional | flops 8154611712 | bytes 20643848 | solution.py:49
  17.0 0.0 copy-start.2
  17.0 1.2 broadcast_select_fusion.3
  18.2 0.0 all-reduce.7.cloned.1.call-update
  18.2 0.0 copy-done.2
  18.2 0.0 all-reduce.5.cloned.1.call-start
  18.3 0.7 all-reduce.5.cloned.1.call-update
  19.0 0.0 all-reduce.11.cloned.1.call-start
  19.1 1.1 slice.16
  20.2 1.1 slice.17
  21.3 207.7 %all-reduce.7.cloned.1.call-done = f32[384,384]{1,0:T(8,128)} async-done(((f32[384,384]{1,0:T(8,128)}), f32[384,384]{1,0:T(8,128)}) %all-reduce.7.cloned.1.call-update) | async-done | bytes 589840 | tf_op jit(solution)/shard_map/psum | solution.py:12
  229.0 121.1 %all-reduce.5.cloned.1.call-done = f32[384,384]{1,0:T(8,128)} async-done(((f32[384,384]{1,0:T(8,128)}), f32[384,384]{1,0:T(8,128)}) %all-reduce.5.cloned.1.call-update) | async-done | bytes 589840 | tf_op jit(solution)/shard_map/psum | solution.py:12
  350.1 5.9 conditional.4
  356.0 0.0 copy-start.4
  356.0 1.1 broadcast_select_fusion
  357.1 0.0 all-reduce.11.cloned.1.call-update
  357.1 0.0 all-reduce.9.cloned.1.call-start
  357.2 0.5 all-reduce.9.cloned.1.call-update
  357.7 215.8 %all-reduce.11.cloned.1.call-done = f32[384,384]{1,0:T(8,128)} async-done(((f32[384,384]{1,0:T(8,128)}), f32[384,384]{1,0:T(8,128)}) %all-reduce.11.cloned.1.call-update) | async-done | bytes 589840 | tf_op jit(solution)/shard_map/psum | solution.py:12
  573.5 120.9 %all-reduce.9.cloned.1.call-done = f32[384,384]{1,0:T(8,128)} async-done(((f32[384,384]{1,0:T(8,128)}), f32[384,384]{1,0:T(8,128)}) %all-reduce.9.cloned.1.call-update) | async-done | bytes 589840 | tf_op jit(solution)/shard_map/psum | solution.py:12
  694.4 0.0 copy-done.4
  694.4 0.0 copy-start.3
  694.4 13.3 %conditional.5 = ((f32[384,384]{1,0:T(8,128)S(1)})) conditional(s32[]{:T(128)} %convert_element_type.16, (f32[384,384]{1,0:T(8,128)S(1)}) %tuple.38, (s32[]{:T(128)}, f32[384,384]{1,0:T(8,128)}, f32[384,384]{1,0:T(8,128)S(1)}, s32[]{:T(128)}, f32[384,384]{1,0:T(8,128)}, /*index=5*/f32[384,768]{1,0:T(8,128)}, f32[384,384]{1,0:T(8,128)S(1)}, ...), branch_computations={%region_8.9_spmd, %region_9.10_spmd} | conditional | flops 2718793728 | bytes 18874484 | solution.py:81
  694.4 4.0 fusion.8
  698.4 0.0 copy-start.7
  698.4 1.3 fusion.29
  699.7 0.0 copy-done.7
  699.7 3.2 convolution_add_fusion.4
  703.0 0.0 copy-start.6
  703.0 0.2 copy.17
  703.2 0.8 copy-done.6
  704.0 3.5 fusion.4
  707.5 0.2 copy.30
  707.7 0.0 copy-done.3
  707.7 0.9 select_select_fusion
  (3 shorter events, 0.1 us)
Async XLA Ops:
  6.5 1.2 copy-start.1
  6.5 1.4 copy-start
  6.5 222.4 %all-reduce.7.cloned.1.call-start = ((), (), s32[]{:S(2)}) async-start(), calls=%async_computation.1 | async-start | bytes 1179648 | tf_op jit(solution)/shard_map/psum | solution.py:12
  17.0 1.2 copy-start.2
  18.2 331.8 %all-reduce.5.cloned.1.call-start = ((), (), s32[]{:S(2)}) async-start(), calls=%async_computation | async-start | bytes 1179648 | tf_op jit(solution)/shard_map/psum | solution.py:12
  19.0 554.5 %all-reduce.11.cloned.1.call-start = ((), (), s32[]{:S(2)}) async-start(), calls=%async_computation.3 | async-start | bytes 1179648 | tf_op jit(solution)/shard_map/psum | solution.py:12
  356.0 338.4 %copy-start.4 = (f32[384,384]{1,0:T(8,128)S(1)}, f32[384,384]{1,0:T(8,128)}, u32[]{:S(2)}) copy-start(f32[384,384]{1,0:T(8,128)} %all-reduce.7.cloned.1.call-done) | copy-start | bytes 1769476
  357.1 337.3 %all-reduce.9.cloned.1.call-start = ((), (), s32[]{:S(2)}) async-start(), calls=%async_computation.2 | async-start | bytes 1179648 | tf_op jit(solution)/shard_map/psum | solution.py:12
  694.4 13.3 %copy-start.3 = (f32[384,384]{1,0:T(8,128)S(1)}, f32[384,384]{1,0:T(8,128)}, u32[]{:S(2)}) copy-start(f32[384,384]{1,0:T(8,128)} %copy-done.2) | copy-start | bytes 1769476
  698.4 1.3 copy-start.7
  703.0 1.1 copy-start.6
Sparse Core Ops, SparseCore 0:
  18.4 210.5 all-reduce.6
  232.2 117.7 all-reduce.4
  357.2 216.2 all-reduce.10
  576.6 117.7 all-reduce.8
where the time goes:
time: 725 us; the launch traced here: 716 us
  waiting for transfers between devices  667 us (92%)
  loops' own time  14.9 us (2%)
  between operations  13.7 us (2%)
  matrix products  12 us (2%)
    psum x4, waiting for transfers between devices, from_root(): return lax.psum(kept, axis)  665 us
  transfers between devices with their start and end apart: 4, of which 4 were waited for; matrix products, arithmetic and copies ran while one was open for 0% of the time, Pallas kernels for 0%

commit v1 on v0

--- a/solution.py
+++ b/solution.py
@@ -9,7 +9,7 @@
 
 def from_root(value, axis, source):
     kept = jnp.where(lax.axis_index(axis) == source, value, 0).astype(value.dtype)
-    return lax.psum(kept, axis)
+    return jnp.sum(lax.all_gather(kept, axis), axis=0)
 
 
 def product(left_side, right_side):

time: 725 us -> 564 us (0.78)
  waiting for transfers between devices: 667 us -> 441 us
  local copies, waits for them, and re-layouts: 5.05 us -> 49.9 us
  other arithmetic: 3.2 us -> 27 us
    psum x4 -> x0, waiting for transfers between devices: 665 us -> none  [from_root(): return lax.psum(kept, axis)]
    all_gather x0 -> x4, waiting for transfers between devices: none -> 440 us  [from_root(): return jnp.sum(lax.all_gather(kept, axis), axis=0)]
    reduce_sum x0 -> x4, other arithmetic: none -> 23.9 us  [from_root(): return jnp.sum(lax.all_gather(kept, axis), axis=0)]
    cond x4 -> x6, local copies, waits for them, and re-layouts: 0.84 us -> 22.8 us
    unnamed x11 -> x15, local copies, waits for them, and re-layouts: 1.43 us -> 22.4 us
  transfers between devices with their start and end apart: 4 -> 4, of which waited for: 4 -> 4; matrix products, arithmetic and copies ran while one was open for 0% -> 2% of each run, Pallas kernels for 0% -> 0%
where the time goes in v1:
time: 564 us; the launch traced here: 554 us
  waiting for transfers between devices  441 us (78%)
  local copies, waits for them, and re-layouts  49.9 us (9%)
  other arithmetic  27 us (5%)
  between operations  13.8 us (2%)
  matrix products  12 us (2%)
  loops' own time  10.5 us (2%)
    all_gather x4, waiting for transfers between devices, from_root(): return jnp.sum(lax.all_gather(kept, axis), axis=0)  440 us
    reduce_sum x4, other arithmetic, from_root(): return jnp.sum(lax.all_gather(kept, axis), axis=0)  23.9 us
    unnamed x15, local copies, waits for them, and re-layouts  22.4 us
    cond x4, local copies, waits for them, and re-layouts  21.5 us
    dot_general x4, matrix products, product(): jnp.dot(left_side, right_side, precision=precise, preferred_element_type=...  12 us
  transfers between devices with their start and end apart: 4, of which 4 were waited for; matrix products, arithmetic and copies ran while one was open for 2% of the time, Pallas kernels for 0%

profile of v1, /device:TPU:102, one launch (start us, length us, event | category | flops | bytes accessed | tf_op | source)
XLA Modules:
  0.0 554.1 jit_solution(16328555725577389227)
XLA Ops:
  6.5 0.0 all-gather.11.cloned.1.call-start
  6.5 1.1 copy.70
  7.6 7.5 %conditional.3 = (f32[384,384]{1,0:T(8,128)S(1)}) conditional(s32[]{:T(128)} %convert_element_type.14, () %tuple.23, (f32[384,384]{1,0:T(8,128)}, f32[384,384]{1,0:T(8,128)S(1)}, f32[384,384]{1,0:T(8,128)}) %tuple.24), branch_computations={%region_0.0_spmd, %region_1.0_spmd} | conditional | flops 8154611712 | bytes 23003172 | solution.py:49
  15.1 0.0 copy-start.4
  15.1 0.2 copy.28
  15.4 1.1 broadcast_select_fusion.3
  16.5 0.0 all-gather.11.cloned.1.call-update
  16.5 0.0 all-gather.9.cloned.1.call-start
  16.6 0.7 all-gather.9.cloned.1.call-update
  17.3 0.0 all-gather.13.cloned.1.call-start
  17.3 1.9 slice.12
  19.3 0.0 copy-done.7
  19.3 0.9 slice.13
  20.2 102.2 %all-gather.11.cloned.1.call-done = f32[6144,384]{0,1:T(8,128)} async-done(((f32[384,384]{0,1:T(8,128)}), f32[6144,384]{0,1:T(8,128)}) %all-gather.11.cloned.1.call-update) | async-done | bytes 9437200 | tf_op jit(solution)/shard_map/all_gather | solution.py:12
  122.4 5.7 %copy.62 = f32[48,8,16,384]{3,2,1,0:T(8,128)S(1)} copy(f32[48,8,16,384]{3,1,2,0:T(8,128)} %bitcast.99) | data formatting | bytes 18874368
  128.1 0.0 copy-done.4
  128.1 2.2 bitcast_reduce_fusion.3
  130.2 110.0 %all-gather.9.cloned.1.call-done = f32[12288,384]{0,1:T(8,128)} async-done(((f32[384,384]{0,1:T(8,128)}), f32[12288,384]{0,1:T(8,128)}) %all-gather.9.cloned.1.call-update) | async-done | bytes 18874384 | tf_op jit(solution)/shard_map/all_gather | solution.py:12
  240.2 15.6 %copy.61 = f32[48,8,32,384]{3,2,1,0:T(8,128)} copy(f32[48,8,32,384]{3,1,2,0:T(8,128)} %bitcast.97) | data formatting | bytes 37748736
  255.9 9.7 %bitcast_reduce_fusion.2 = f32[384,384]{0,1:T(8,128)S(1)} fusion(f32[48,8,32,384]{3,2,1,0:T(8,128)} %copy.61), kind=kLoop, calls=%fused_computation.38 | loop fusion | flops 4571136 | bytes 19464192 | tf_op jit(solution)/shard_map/reduce_sum | solution.py:12
  265.5 0.9 broadcast_in_dim.17
  266.4 0.0 copy-done
  266.4 0.0 copy-done.1
  266.4 2.7 conditional.4
  269.1 1.1 broadcast_select_fusion
  270.2 0.0 all-gather.13.cloned.1.call-update
  270.3 0.0 all-gather.15.cloned.1.call-start
  270.3 0.5 all-gather.15.cloned.1.call-update
  270.8 1.1 copy.40
  271.9 109.6 %all-gather.13.cloned.1.call-done = f32[6144,384]{0,1:T(8,128)} async-done(((f32[384,384]{0,1:T(8,128)}), f32[6144,384]{0,1:T(8,128)}) %all-gather.13.cloned.1.call-update) | async-done | bytes 9437200 | tf_op jit(solution)/shard_map/all_gather | solution.py:12
  381.5 117.7 %all-gather.15.cloned.1.call-done = f32[12288,384]{0,1:T(8,128)} async-done(((f32[384,384]{0,1:T(8,128)}), f32[12288,384]{0,1:T(8,128)}) %all-gather.15.cloned.1.call-update) | async-done | bytes 18874384 | tf_op jit(solution)/shard_map/all_gather | solution.py:12
  499.2 46.9 %conditional.5 = ((f32[384,384]{1,0:T(8,128)S(1)})) conditional(s32[]{:T(128)} %convert_element_type.16, (f32[384,384]{1,0:T(8,128)S(1)}) %tuple.36, (s32[]{:T(128)}, f32[384,384]{0,1:T(8,128)S(1)}, f32[384,384]{1,0:T(8,128)}, s32[]{:T(128)}, f32[6144,384]{0,1:T(8,128)}, /*index=5*/f32[384,768]{1,0:T(8,128)}, f32[384,384]{0,1:T(8,128)S(1)}, ...), branch_computations={%region_8.9_spmd, %region_9.10_spmd.clone} | conditional | flops 2725576704 | bytes 102629472 | solution.py:81
  499.2 0.2 copy.55
  499.4 4.0 fusion.14
  503.5 15.9 %copy.60 = f32[48,8,32,384]{3,2,1,0:T(8,128)} copy(f32[48,8,32,384]{3,1,2,0:T(8,128)} %bitcast.96) | data formatting | bytes 37748736 | tf_op jit(solution)/shard_map/cond
  519.4 9.6 %bitcast_reduce_fusion = f32[384,384]{0,1:T(8,128)S(1)} fusion(f32[]{:T(128)} %get-tuple-element.169, f32[48,8,32,384]{3,2,1,0:T(8,128)} %copy.60), kind=kLoop, calls=%fused_computation.20 | loop fusion | flops 4571136 | bytes 19464196 | tf_op jit(solution)/shard_map/reduce_sum | solution.py:12
  529.0 0.0 copy-done.3
  529.0 1.3 fusion.36
  530.3 3.2 convolution_add_fusion.8
  533.5 5.6 %copy.59 = f32[48,8,16,384]{3,2,1,0:T(8,128)S(1)} copy(f32[48,8,16,384]{3,1,2,0:T(8,128)} %bitcast.98) | data formatting | bytes 18874368 | tf_op jit(solution)/shard_map/cond
  539.1 2.4 bitcast_reduce_fusion.1
  541.6 0.2 copy.56
  541.8 0.2 copy.57
  542.1 3.5 fusion.10
  545.5 0.2 copy.58
  546.1 0.0 copy-done.5
  546.1 0.0 copy-done.6
  546.1 0.9 select_select_fusion
  (8 shorter events, 0.1 us)
Async XLA Ops:
  6.5 115.8 %all-gather.11.cloned.1.call-start = ((), (), s32[]{:S(2)}) async-start(), calls=%async_computation.1 | async-start | bytes 10027008 | tf_op jit(solution)/shard_map/all_gather | solution.py:12
  7.6 11.7 %copy-start.7 = (f32[768,384]{1,0:T(8,128)S(1)}, f32[768,384]{1,0:T(8,128)}, u32[]{:S(2)}) copy-start(f32[768,384]{1,0:T(8,128)} %param.13) | copy-start | bytes 3538948
  15.1 112.9 %copy-start.4 = (f32[384,384]{1,0:T(8,128)}, f32[384,384]{1,0:T(8,128)S(1)}, u32[]{:S(2)}) copy-start(f32[384,384]{1,0:T(8,128)S(1)} %get-tuple-element.205) | copy-start | bytes 1769476
  16.5 223.7 %all-gather.9.cloned.1.call-start = ((), (), s32[]{:S(2)}) async-start(), calls=%async_computation | async-start | bytes 19464192 | tf_op jit(solution)/shard_map/all_gather | solution.py:12
  17.3 364.2 %all-gather.13.cloned.1.call-start = ((), (), s32[]{:S(2)}) async-start(), calls=%async_computation.2 | async-start | bytes 10027008 | tf_op jit(solution)/shard_map/all_gather | solution.py:12
  255.9 10.5 %copy-start = (f32[384,384]{1,0:T(8,128)S(1)}, f32[384,384]{1,0:T(8,128)}, u32[]{:S(2)}) copy-start(f32[384,384]{1,0:T(8,128)} %param.15) | copy-start | bytes 1769476
  255.9 10.5 %copy-start.1 = (f32[384,384]{1,0:T(8,128)S(1)}, f32[384,384]{1,0:T(8,128)}, u32[]{:S(2)}) copy-start(f32[384,384]{1,0:T(8,128)} %param.14) | copy-start | bytes 1769476
  270.3 228.9 %all-gather.15.cloned.1.call-start = ((), (), s32[]{:S(2)}) async-start(), calls=%async_computation.3 | async-start | bytes 19464192 | tf_op jit(solution)/shard_map/all_gather | solution.py:12
  499.2 46.9 %copy-start.5 = (f32[384,384]{1,0:T(8,128)S(1)}, f32[384,384]{1,0:T(8,128)}, u32[]{:S(2)}) copy-start(f32[384,384]{1,0:T(8,128)} %copy-done.4) | copy-start | bytes 1769476
  499.2 46.9 %copy-start.6 = (f32[384,384]{1,0:T(8,128)S(1)}, f32[384,384]{1,0:T(8,128)}, u32[]{:S(2)}) copy-start(f32[384,384]{1,0:T(8,128)} %copy.40) | copy-start | bytes 1769476
  519.4 9.6 %copy-start.3 = (f32[384,384]{1,0:T(8,128)S(1)}, f32[384,384]{1,0:T(8,128)}, u32[]{:S(2)}) copy-start(f32[384,384]{1,0:T(8,128)} %get-tuple-element.167) | copy-start | bytes 1769476 | tf_op jit(solution)/shard_map/cond
Sparse Core Ops, SparseCore 0:
  16.7 105.6 all-gather.10
  124.5 115.6 all-gather.8
  270.4 111.0 all-gather.12
  383.5 115.6 all-gather.14
